TPU v7x, 128 devices: a whole 4x4x4 slice. The times are simulated.
128 devices in a mesh: pipe: 4 (over z), expert: 32 (over x, y, core).
Axes of the slice: x: 4, y: 4, z: 4, core: 2. Of those that a mesh axis runs over, the one named last changes fastest.
Arguments:
- down_tokens: bfloat16 [2, 1024, 3584], P(None, 'expert'), may hold values from -6 to 6
- up_tokens: bfloat16 [2, 1024, 3584], P(None, 'expert'), may hold values from -6 to 6
- norm_gain: float32 [4, 3584], P('pipe'), may hold values from 0.1 to 1.9
- w_gate: bfloat16 [4, 32, 3584, 1024], P('pipe', 'expert'), may hold values from -0.09375 to 0.09375
- w_up: bfloat16 [4, 32, 3584, 1024], P('pipe', 'expert'), may hold values from -0.09375 to 0.09375
- w_down: bfloat16 [4, 32, 1024, 3584], P('pipe', 'expert'), may hold values from -0.1875 to 0.1875
- down_ids: int32 [4, 2, 1024, 8], P('pipe', None, 'expert'), may hold values from 0 to 31, all different within a row; in each aligned block of 32 rows (0 to 31, 32 to 63, ..., all dimensions but the last counted through in order) at most 10 rows name the same one
- down_gates: float32 [4, 2, 1024, 8], P('pipe', None, 'expert'), may hold values from 0.1 to 1
- up_ids: int32 [4, 2, 1024, 8], P('pipe', None, 'expert'), may hold values from 0 to 31, all different within a row; in each aligned block of 32 rows (0 to 31, 32 to 63, ..., all dimensions but the last counted through in order) at most 10 rows name the same one
- up_gates: float32 [4, 2, 1024, 8], P('pipe', None, 'expert'), may hold values from 0.1 to 1
- key_cotangent: bfloat16 [4, 2, 2, 1024, 64], P('pipe', None, None, 'expert'), may hold values from -0.119628906 to 0.119628906
Outputs:
- down_states: bfloat16 [4, 2, 1024, 3584], P('pipe', None, 'expert')
- up_states: bfloat16 [4, 2, 1024, 3584], P('pipe', None, 'expert')
- kr_grad: float32 [4, 3584, 64], P('pipe', 'expert')
Inputs may be any that keep to these rules, and one draw needn't show every extreme that they name: `down_ids`: each row names 8 different experts. Among the 32 rows of one device in one micro-batch at one section, no expert is named more than 10 times, a bound that some block reaches. `up_ids`: each row names 8 different experts. Among the 32 rows of one device in one micro-batch at one section, no expert is named more than 10 times, a bound that some block reaches.
All inputs are finite; a program needn't handle non-finite values.
Results may differ from a plain program's by a relative error of at most 0.017.
Values may be sent and summed in bfloat16 or wider, within the bound.
No kernel may reach another device: no remote copies, remote signals or barrier semaphores. Data moves between devices by JAX's collectives and lax.ppermute only.
A program may use at most 128 MiB of HBM per device.

v0:
```python
from functools import partial

import jax
import jax.numpy as jnp
from jax import lax
from jax.sharding import PartitionSpec as P

EPSILON = 1e-06


def passed_along(value, axis, steps):
    count = lax.axis_size(axis)
    first, last = (max(0, -steps), min(count, count - steps))
    return lax.ppermute(value, axis, [(source, source + steps) for source in range(first, last)])


def normalize(carried, norm_scale):
    values = carried.astype(jnp.float32)
    inv_rms = lax.rsqrt(jnp.mean(values * values, axis=-1, keepdims=True) + EPSILON)
    return (values * inv_rms * norm_scale).astype(jnp.bfloat16)


def expert_rows(row_block, gate_mat, up_mat, down_mat):
    gate_act = jnp.dot(row_block, gate_mat, preferred_element_type=jnp.float32)
    up_act = jnp.dot(row_block, up_mat, preferred_element_type=jnp.float32)
    hidden = (jax.nn.silu(gate_act) * up_act).astype(jnp.bfloat16)
    return jnp.dot(hidden, down_mat, preferred_element_type=jnp.float32).astype(jnp.bfloat16)


def apply_expert(row_block, weights):
    return expert_rows(row_block, weights[0], weights[1], weights[2])


def slot_layout(route_ids, expert_count, capacity):
    expert_axis = jnp.arange(expert_count, dtype=jnp.int32)
    chosen = jnp.sum((route_ids[:, :, None] == expert_axis).astype(jnp.int32), axis=1)
    slot_rank = jnp.cumsum(chosen, axis=0) - 1
    slot_axis = jnp.arange(capacity, dtype=jnp.int32)
    return chosen[:, :, None] * (slot_rank[:, :, None] == slot_axis).astype(jnp.int32)


def run_layer(carried, norm_scale, weights, route_ids, route_gates, active):
    normed = normalize(carried, norm_scale)
    expert_count = lax.axis_size("expert")
    token_count, pick_count = route_ids.shape
    capacity = min(token_count, 5 * token_count * pick_count // (4 * expert_count))
    slot_table = slot_layout(route_ids, expert_count, capacity)
    outgoing = jnp.einsum(
        "tec,td->ecd", slot_table.astype(jnp.bfloat16), normed, preferred_element_type=jnp.float32
    ).astype(jnp.bfloat16)
    arrived = lax.all_to_all(outgoing, "expert", split_axis=0, concat_axis=0, tiled=True)
    source_count, item_count, feature_count = arrived.shape
    row_block = arrived.reshape(source_count * item_count, feature_count)
    finished = lax.cond(active, partial(apply_expert, weights=weights), jnp.zeros_like, row_block)
    returned = lax.all_to_all(
        finished.reshape(source_count, item_count, feature_count),
        "expert",
        split_axis=0,
        concat_axis=0,
        tiled=True,
    )
    expert_axis = jnp.arange(expert_count, dtype=jnp.int32)
    gate_weight = jnp.sum(
        route_gates[:, :, None] * (route_ids[:, :, None] == expert_axis).astype(jnp.float32), axis=1
    )
    weighted = (slot_table.astype(jnp.float32) * gate_weight[:, :, None]).reshape(
        token_count, expert_count * capacity
    )
    flat_returned = returned.reshape(expert_count * capacity, returned.shape[2]).astype(jnp.float32)
    combined = jnp.dot(weighted, flat_returned, precision=lax.Precision.HIGHEST)
    output = (carried.astype(jnp.float32) + combined).astype(jnp.bfloat16)
    return (output, normed)


def pass_on(values):
    to_next = passed_along(values, "pipe", 1)
    behind = passed_along(values, "pipe", -1)
    return (to_next, behind)


def grad_term(row_source, tangents):
    return jnp.einsum("td,tr->dr", row_source, tangents, preferred_element_type=jnp.float32)


def on_device(
    down_tokens,
    up_tokens,
    norm_gain,
    w_gate,
    w_up,
    w_down,
    down_ids,
    down_gates,
    up_ids,
    up_gates,
    key_cotangent,
):
    segment_count = lax.axis_size("pipe")
    expert_count = lax.axis_size("expert")
    segment_pos = lax.axis_index("pipe")
    micro_count = down_tokens.shape[0]
    feature_count = down_tokens.shape[2]
    rope_width = key_cotangent.shape[4]
    own_rows = feature_count // expert_count
    norm_scale = norm_gain[0]
    weights = (w_gate[0, 0], w_up[0, 0], w_down[0, 0])
    total_steps = segment_count + 2 * micro_count - 2
    from_prior = jnp.zeros_like(down_tokens[0])
    from_next = jnp.zeros_like(up_tokens[0])
    down_states = jnp.zeros_like(down_tokens)
    up_states = jnp.zeros_like(up_tokens)
    key_grad_acc = jnp.zeros((own_rows, rope_width), jnp.float32)
    micro_slots = jnp.arange(micro_count, dtype=jnp.int32)
    for step_index in range(total_steps):
        lag_down = step_index - segment_pos
        lag_up = step_index - (segment_count - 1 - segment_pos)
        down_on = (lag_down >= 0) & (lag_down % 2 == 0) & (lag_down < 2 * micro_count)
        up_on = (lag_up >= 0) & (lag_up % 2 == 0) & (lag_up < 2 * micro_count)
        down_mb = jnp.clip(lag_down // 2, 0, micro_count - 1)
        up_mb = jnp.clip(lag_up // 2, 0, micro_count - 1)
        down_in = jnp.where(segment_pos == 0, down_tokens[down_mb], from_prior)
        up_in = jnp.where(segment_pos == segment_count - 1, up_tokens[up_mb], from_next)
        carried = jnp.where(down_on, down_in, up_in)
        route_ids = jnp.where(down_on, down_ids[0, down_mb], up_ids[0, up_mb])
        route_gates = jnp.where(down_on, down_gates[0, down_mb], up_gates[0, up_mb])
        active = down_on | up_on
        output, normed = run_layer(carried, norm_scale, weights, route_ids, route_gates, active)
        down_states = jnp.where(
            (micro_slots == down_mb)[:, None, None] & down_on, output[None], down_states
        )
        up_states = jnp.where(
            (micro_slots == up_mb)[:, None, None] & up_on, output[None], up_states
        )
        tangent = jnp.where(down_on, key_cotangent[0, 0, down_mb], key_cotangent[0, 1, up_mb])
        tangent = tangent * active.astype(tangent.dtype)
        key_grad_acc = key_grad_acc + lax.psum_scatter(
            grad_term(normed, tangent).astype(jnp.bfloat16),
            "expert",
            scatter_dimension=0,
            tiled=True,
        ).astype(jnp.float32)
        if step_index + 1 < total_steps:
            from_prior, from_next = pass_on(output)
    return (down_states[None], up_states[None], key_grad_acc[None])


def solution(mesh):
    return jax.shard_map(
        on_device,
        mesh=mesh,
        in_specs=(
            P(None, "expert", None),
            P(None, "expert", None),
            P("pipe", None),
            P("pipe", "expert", None, None),
            P("pipe", "expert", None, None),
            P("pipe", "expert", None, None),
            P("pipe", None, "expert", None),
            P("pipe", None, "expert", None),
            P("pipe", None, "expert", None),
            P("pipe", None, "expert", None),
            P("pipe", None, None, "expert", None),
        ),
        out_specs=(
            P("pipe", None, "expert", None),
            P("pipe", None, "expert", None),
            P("pipe", "expert", None),
        ),
        check_vma=False,
    )
```

profile of v0, /device:TPU:0, one launch (start us, length us, event | category | flops | bytes accessed | tf_op | source)
XLA Modules:
  0.0 1219.5 jit_solution(13113218519188460712)
XLA Ops:
  15.3 7.5 all-to-all-start
  22.9 46.1 %all-to-all-done = bf16[32,10,3584]{2,1,0:T(8,128)(2,1)} async-done(((bf16[32,10,3584]{2,1,0:T(8,128)(2,1)}), bf16[32,10,3584]{2,1,0:T(8,128)(2,1)}, u32[]{:S(2)}, u32[]{:S(2)}) %all-to-all-start) | async-done | bytes 2293792 | tf_op jit(solution)/shard_map/all_to_all | solution.py:51
  69.0 22.3 %conditional.6 = (bf16[320,3584]{1,0:T(8,128)(2,1)S(1)}) conditional(s32[]{:T(128)} %convert_element_type.273, () %tuple.44, (bf16[32,10,3584]{2,1,0:T(8,128)(2,1)}, bf16[3584,1024]{1,0:T(8,128)(2,1)}, bf16[3584,1024]{1,0:T(8,128)(2,1)}, bf16[1024,3584]{1,0:T(8,128)(2,1)}) %tuple.123), branch_computations={%region_4.5_spmd, %region_5.6_spmd} | conditional | flops 7049543680 | bytes 45285412 | solution.py:54
  73.5 6.7 fusion.217
  80.2 11.2 convolution_convert_fusion
  93.9 6.9 all-to-all-start.1
  101.8 45.2 %all-to-all-done.1 = bf16[32,10,3584]{2,1,0:T(8,128)(2,1)} async-done(((bf16[32,10,3584]{2,1,0:T(8,128)(2,1)}), bf16[32,10,3584]{2,1,0:T(8,128)(2,1)}, u32[]{:S(2)}, u32[]{:S(2)}) %all-to-all-start.1) | async-done | bytes 2293792 | tf_op jit(solution)/shard_map/all_to_all | solution.py:55
  172.9 46.1 %all-to-all-done.2 = bf16[32,10,3584]{2,1,0:T(8,128)(2,1)} async-done(((bf16[32,10,3584]{2,1,0:T(8,128)(2,1)}), bf16[32,10,3584]{2,1,0:T(8,128)(2,1)}, u32[]{:S(2)}, u32[]{:S(2)}) %all-to-all-start.2) | async-done | bytes 2293792 | tf_op jit(solution)/shard_map/all_to_all | solution.py:51
  228.7 45.8 %all-to-all-done.3 = bf16[32,10,3584]{2,1,0:T(8,128)(2,1)} async-done(((bf16[32,10,3584]{2,1,0:T(8,128)(2,1)}), bf16[32,10,3584]{2,1,0:T(8,128)(2,1)}, u32[]{:S(2)}, u32[]{:S(2)}) %all-to-all-start.3) | async-done | bytes 2293792 | tf_op jit(solution)/shard_map/all_to_all | solution.py:55
  280.4 27.2 %collective-permute-start.2 = (bf16[32,3584]{1,0:T(8,128)(2,1)S(1)}, bf16[32,3584]{1,0:T(8,128)(2,1)S(1)}, u32[]{:S(2)}, u32[]{:S(2)}) collective-permute-start(bf16[32,3584]{1,0:T(8,128)(2,1)S(1)} %fusion.22), channel_id=1, source_target_pairs={{0,32},{32,64},{64,96},{1,33},{33,65},{65,97},{2,34},{34,66},{66,9... | collective-permute-start | bytes 688136 | tf_op jit(solution)/shard_map/ppermute | solution.py:14
  323.4 46.1 %all-to-all-done.4 = bf16[32,10,3584]{2,1,0:T(8,128)(2,1)} async-done(((bf16[32,10,3584]{2,1,0:T(8,128)(2,1)}), bf16[32,10,3584]{2,1,0:T(8,128)(2,1)}, u32[]{:S(2)}, u32[]{:S(2)}) %all-to-all-start.4) | async-done | bytes 2293792 | tf_op jit(solution)/shard_map/all_to_all | solution.py:51
  369.5 22.3 %conditional.8 = (bf16[320,3584]{1,0:T(8,128)(2,1)S(1)}) conditional(s32[]{:T(128)} %convert_element_type.289, () %tuple.48, (bf16[32,10,3584]{2,1,0:T(8,128)(2,1)}, bf16[3584,1024]{1,0:T(8,128)(2,1)}, bf16[3584,1024]{1,0:T(8,128)(2,1)}, bf16[1024,3584]{1,0:T(8,128)(2,1)}) %tuple.125), branch_computations={%region_16.17_spmd, %region_17.18_spmd} | conditional | flops 7049543680 | bytes 45285412 | solution.py:54
  380.7 11.2 convolution_convert_fusion.2
  401.4 45.9 %all-to-all-done.5 = bf16[32,10,3584]{2,1,0:T(8,128)(2,1)} async-done(((bf16[32,10,3584]{2,1,0:T(8,128)(2,1)}), bf16[32,10,3584]{2,1,0:T(8,128)(2,1)}, u32[]{:S(2)}, u32[]{:S(2)}) %all-to-all-start.5) | async-done | bytes 2293792 | tf_op jit(solution)/shard_map/all_to_all | solution.py:55
  473.9 46.1 %all-to-all-done.6 = bf16[32,10,3584]{2,1,0:T(8,128)(2,1)} async-done(((bf16[32,10,3584]{2,1,0:T(8,128)(2,1)}), bf16[32,10,3584]{2,1,0:T(8,128)(2,1)}, u32[]{:S(2)}, u32[]{:S(2)}) %all-to-all-start.6) | async-done | bytes 2293792 | tf_op jit(solution)/shard_map/all_to_all | solution.py:51
  520.0 22.3 %conditional.9 = (bf16[320,3584]{1,0:T(8,128)(2,1)S(1)}) conditional(s32[]{:T(128)} %convert_element_type.297, () %tuple.50, (bf16[32,10,3584]{2,1,0:T(8,128)(2,1)}, bf16[3584,1024]{1,0:T(8,128)(2,1)}, bf16[3584,1024]{1,0:T(8,128)(2,1)}, bf16[1024,3584]{1,0:T(8,128)(2,1)}) %tuple.126), branch_computations={%region_22.23_spmd, %region_23.24_spmd} | conditional | flops 7049543680 | bytes 45285412 | solution.py:54
  524.5 6.7 fusion.220
  531.2 11.2 convolution_convert_fusion.3
  545.0 6.8 all-to-all-start.7
  552.2 45.8 %all-to-all-done.7 = bf16[32,10,3584]{2,1,0:T(8,128)(2,1)} async-done(((bf16[32,10,3584]{2,1,0:T(8,128)(2,1)}), bf16[32,10,3584]{2,1,0:T(8,128)(2,1)}, u32[]{:S(2)}, u32[]{:S(2)}) %all-to-all-start.7) | async-done | bytes 2293792 | tf_op jit(solution)/shard_map/all_to_all | solution.py:55
  624.6 46.1 %all-to-all-done.8 = bf16[32,10,3584]{2,1,0:T(8,128)(2,1)} async-done(((bf16[32,10,3584]{2,1,0:T(8,128)(2,1)}), bf16[32,10,3584]{2,1,0:T(8,128)(2,1)}, u32[]{:S(2)}, u32[]{:S(2)}) %all-to-all-start.8) | async-done | bytes 2293792 | tf_op jit(solution)/shard_map/all_to_all | solution.py:51
  682.2 43.8 %all-to-all-done.9 = bf16[32,10,3584]{2,1,0:T(8,128)(2,1)} async-done(((bf16[32,10,3584]{2,1,0:T(8,128)(2,1)}), bf16[32,10,3584]{2,1,0:T(8,128)(2,1)}, u32[]{:S(2)}, u32[]{:S(2)}) %all-to-all-start.9) | async-done | bytes 2293792 | tf_op jit(solution)/shard_map/all_to_all | solution.py:55
  732.0 27.3 %collective-permute-start.8 = (bf16[32,3584]{1,0:T(8,128)(2,1)S(1)}, bf16[32,3584]{1,0:T(8,128)(2,1)S(1)}, u32[]{:S(2)}, u32[]{:S(2)}) collective-permute-start(bf16[32,3584]{1,0:T(8,128)(2,1)S(1)} %fusion.19), channel_id=1, source_target_pairs={{0,32},{32,64},{64,96},{1,33},{33,65},{65,97},{2,34},{34,66},{66,9... | collective-permute-start | bytes 688136 | tf_op jit(solution)/shard_map/ppermute | solution.py:14
  779.7 41.2 %all-to-all-done.10 = bf16[32,10,3584]{2,1,0:T(8,128)(2,1)} async-done(((bf16[32,10,3584]{2,1,0:T(8,128)(2,1)}), bf16[32,10,3584]{2,1,0:T(8,128)(2,1)}, u32[]{:S(2)}, u32[]{:S(2)}) %all-to-all-start.10) | async-done | bytes 2293792 | tf_op jit(solution)/shard_map/all_to_all | solution.py:51
  820.9 22.7 %conditional.11 = (bf16[320,3584]{1,0:T(8,128)(2,1)S(1)}) conditional(s32[]{:T(128)} %convert_element_type.313, () %tuple.54, (bf16[32,10,3584]{2,1,0:T(8,128)(2,1)}, bf16[3584,1024]{1,0:T(8,128)(2,1)}, bf16[3584,1024]{1,0:T(8,128)(2,1)}, bf16[1024,3584]{1,0:T(8,128)(2,1)}) %tuple.128), branch_computations={%region_34.35_spmd, %region_35.36_spmd} | conditional | flops 7049543680 | bytes 45285412 | solution.py:54
  825.7 6.7 fusion.222
  832.3 11.3 convolution_convert_fusion.5
  857.3 45.0 %reduce-scatter.21.cloned.1.call-done = bf16[112,64]{1,0:T(8,128)(2,1)} async-done(((bf16[3584,64]{1,0:T(8,128)(2,1)}), bf16[112,64]{1,0:T(8,128)(2,1)}) %reduce-scatter.21.cloned.1.call-update) | async-done | bytes 14352
  903.1 75.3 %reduce-scatter.23.cloned.1.call-done = bf16[112,64]{1,0:T(8,128)(2,1)} async-done(((bf16[3584,64]{1,0:T(8,128)(2,1)}), bf16[112,64]{1,0:T(8,128)(2,1)}) %reduce-scatter.23.cloned.1.call-update) | async-done | bytes 14352
  979.2 74.7 %reduce-scatter.25.cloned.1.call-done = bf16[112,64]{1,0:T(8,128)(2,1)} async-done(((bf16[3584,64]{1,0:T(8,128)(2,1)}), bf16[112,64]{1,0:T(8,128)(2,1)}) %reduce-scatter.25.cloned.1.call-update) | async-done | bytes 14352
  1054.8 74.7 %reduce-scatter.27.cloned.1.call-done = bf16[112,64]{1,0:T(8,128)(2,1)} async-done(((bf16[3584,64]{1,0:T(8,128)(2,1)}), bf16[112,64]{1,0:T(8,128)(2,1)}) %reduce-scatter.27.cloned.1.call-update) | async-done | bytes 14352
  1130.3 74.7 %reduce-scatter.29.cloned.1.call-done = bf16[112,64]{1,0:T(8,128)(2,1)} async-done(((bf16[3584,64]{1,0:T(8,128)(2,1)}), bf16[112,64]{1,0:T(8,128)(2,1)}) %reduce-scatter.29.cloned.1.call-update) | async-done | bytes 14352
  (248 shorter events, 220.4 us)
Async XLA Ops:
  15.3 53.7 %all-to-all-start = ((bf16[32,10,3584]{2,1,0:T(8,128)(2,1)}), bf16[32,10,3584]{2,1,0:T(8,128)(2,1)}, u32[]{:S(2)}, u32[]{:S(2)}) async-start(bf16[32,10,3584]{2,1,0:T(8,128)(2,1)} %copy.101), calls=%async_computation | async-start | bytes 7340032 | tf_op jit(solution)/shard_map/all_to_all | solution.py:51
  93.9 53.0 %all-to-all-start.1 = ((bf16[32,10,3584]{2,1,0:T(8,128)(2,1)}), bf16[32,10,3584]{2,1,0:T(8,128)(2,1)}, u32[]{:S(2)}, u32[]{:S(2)}) async-start(bf16[32,10,3584]{2,1,0:T(8,128)(2,1)} %reshape.453), calls=%async_computation.1 | async-start | bytes 7340032 | tf_op jit(solution)/shard_map/all_to_all | solution.py:55
  151.6 9.1 collective-permute-start.1
  152.9 9.0 collective-permute-start
  166.8 52.2 %all-to-all-start.2 = ((bf16[32,10,3584]{2,1,0:T(8,128)(2,1)}), bf16[32,10,3584]{2,1,0:T(8,128)(2,1)}, u32[]{:S(2)}, u32[]{:S(2)}) async-start(bf16[32,10,3584]{2,1,0:T(8,128)(2,1)} %copy.106), calls=%async_computation.2 | async-start | bytes 7340032 | tf_op jit(solution)/shard_map/all_to_all | solution.py:51
  221.8 52.7 %all-to-all-start.3 = ((bf16[32,10,3584]{2,1,0:T(8,128)(2,1)}), bf16[32,10,3584]{2,1,0:T(8,128)(2,1)}, u32[]{:S(2)}, u32[]{:S(2)}) async-start(bf16[32,10,3584]{2,1,0:T(8,128)(2,1)} %reshape.454), calls=%async_computation.3 | async-start | bytes 7340032 | tf_op jit(solution)/shard_map/all_to_all | solution.py:55
  279.1 32.0 %collective-permute-start.3 = (bf16[32,3584]{1,0:T(8,128)(2,1)S(1)}, bf16[32,3584]{1,0:T(8,128)(2,1)S(1)}, u32[]{:S(2)}, u32[]{:S(2)}) collective-permute-start(bf16[32,3584]{1,0:T(8,128)(2,1)S(1)} %fusion.22), channel_id=1, source_target_pairs={{32,0},{64,32},{96,64},{33,1},{65,33},{97,65},{34,2},{66,34},{98,6... | collective-permute-start | bytes 688136 | tf_op jit(solution)/shard_map/ppermute | solution.py:14
  280.4 31.9 %collective-permute-start.2 = (bf16[32,3584]{1,0:T(8,128)(2,1)S(1)}, bf16[32,3584]{1,0:T(8,128)(2,1)S(1)}, u32[]{:S(2)}, u32[]{:S(2)}) collective-permute-start(bf16[32,3584]{1,0:T(8,128)(2,1)S(1)} %fusion.22), channel_id=1, source_target_pairs={{0,32},{32,64},{64,96},{1,33},{33,65},{65,97},{2,34},{34,66},{66,9... | collective-permute-start | bytes 688136 | tf_op jit(solution)/shard_map/ppermute | solution.py:14
  317.3 52.2 %all-to-all-start.4 = ((bf16[32,10,3584]{2,1,0:T(8,128)(2,1)}), bf16[32,10,3584]{2,1,0:T(8,128)(2,1)}, u32[]{:S(2)}, u32[]{:S(2)}) async-start(bf16[32,10,3584]{2,1,0:T(8,128)(2,1)} %copy.111), calls=%async_computation.4 | async-start | bytes 7340032 | tf_op jit(solution)/shard_map/all_to_all | solution.py:51
  394.5 52.8 %all-to-all-start.5 = ((bf16[32,10,3584]{2,1,0:T(8,128)(2,1)}), bf16[32,10,3584]{2,1,0:T(8,128)(2,1)}, u32[]{:S(2)}, u32[]{:S(2)}) async-start(bf16[32,10,3584]{2,1,0:T(8,128)(2,1)} %reshape.455), calls=%async_computation.5 | async-start | bytes 7340032 | tf_op jit(solution)/shard_map/all_to_all | solution.py:55
  451.9 9.8 collective-permute-start.5
  453.2 9.7 collective-permute-start.4
  467.8 52.2 %all-to-all-start.6 = ((bf16[32,10,3584]{2,1,0:T(8,128)(2,1)}), bf16[32,10,3584]{2,1,0:T(8,128)(2,1)}, u32[]{:S(2)}, u32[]{:S(2)}) async-start(bf16[32,10,3584]{2,1,0:T(8,128)(2,1)} %copy.116), calls=%async_computation.6 | async-start | bytes 7340032 | tf_op jit(solution)/shard_map/all_to_all | solution.py:51
  545.0 53.0 %all-to-all-start.7 = ((bf16[32,10,3584]{2,1,0:T(8,128)(2,1)}), bf16[32,10,3584]{2,1,0:T(8,128)(2,1)}, u32[]{:S(2)}, u32[]{:S(2)}) async-start(bf16[32,10,3584]{2,1,0:T(8,128)(2,1)} %reshape.456), calls=%async_computation.7 | async-start | bytes 7340032 | tf_op jit(solution)/shard_map/all_to_all | solution.py:55
  602.6 9.8 collective-permute-start.7
  603.9 9.7 collective-permute-start.6
  618.5 52.2 %all-to-all-start.8 = ((bf16[32,10,3584]{2,1,0:T(8,128)(2,1)}), bf16[32,10,3584]{2,1,0:T(8,128)(2,1)}, u32[]{:S(2)}, u32[]{:S(2)}) async-start(bf16[32,10,3584]{2,1,0:T(8,128)(2,1)} %copy.121), calls=%async_computation.8 | async-start | bytes 7340032 | tf_op jit(solution)/shard_map/all_to_all | solution.py:51
  673.5 52.6 %all-to-all-start.9 = ((bf16[32,10,3584]{2,1,0:T(8,128)(2,1)}), bf16[32,10,3584]{2,1,0:T(8,128)(2,1)}, u32[]{:S(2)}, u32[]{:S(2)}) async-start(bf16[32,10,3584]{2,1,0:T(8,128)(2,1)} %reshape.457), calls=%async_computation.9 | async-start | bytes 7340032 | tf_op jit(solution)/shard_map/all_to_all | solution.py:55
  679.9 176.5 %reduce-scatter.19.cloned.1.call-start = ((), (), s32[]{:S(2)}) async-start(), calls=%async_computation.18 | async-start | bytes 946176
  730.7 32.2 %collective-permute-start.9 = (bf16[32,3584]{1,0:T(8,128)(2,1)S(1)}, bf16[32,3584]{1,0:T(8,128)(2,1)S(1)}, u32[]{:S(2)}, u32[]{:S(2)}) collective-permute-start(bf16[32,3584]{1,0:T(8,128)(2,1)S(1)} %fusion.19), channel_id=1, source_target_pairs={{32,0},{64,32},{96,64},{33,1},{65,33},{97,65},{34,2},{66,34},{98,6... | collective-permute-start | bytes 688136 | tf_op jit(solution)/shard_map/ppermute | solution.py:14
  732.0 32.0 %collective-permute-start.8 = (bf16[32,3584]{1,0:T(8,128)(2,1)S(1)}, bf16[32,3584]{1,0:T(8,128)(2,1)S(1)}, u32[]{:S(2)}, u32[]{:S(2)}) collective-permute-start(bf16[32,3584]{1,0:T(8,128)(2,1)S(1)} %fusion.19), channel_id=1, source_target_pairs={{0,32},{32,64},{64,96},{1,33},{33,65},{65,97},{2,34},{34,66},{66,9... | collective-permute-start | bytes 688136 | tf_op jit(solution)/shard_map/ppermute | solution.py:14
  768.3 52.6 %all-to-all-start.10 = ((bf16[32,10,3584]{2,1,0:T(8,128)(2,1)}), bf16[32,10,3584]{2,1,0:T(8,128)(2,1)}, u32[]{:S(2)}, u32[]{:S(2)}) async-start(bf16[32,10,3584]{2,1,0:T(8,128)(2,1)} %copy.126), calls=%async_computation.10 | async-start | bytes 7340032 | tf_op jit(solution)/shard_map/all_to_all | solution.py:51
  774.5 127.8 %reduce-scatter.21.cloned.1.call-start = ((), (), s32[]{:S(2)}) async-start(), calls=%async_computation.19 | async-start | bytes 946176
  776.2 202.2 %reduce-scatter.23.cloned.1.call-start = ((), (), s32[]{:S(2)}) async-start(), calls=%async_computation.20 | async-start | bytes 946176
  777.9 276.0 %reduce-scatter.25.cloned.1.call-start = ((), (), s32[]{:S(2)}) async-start(), calls=%async_computation.21 | async-start | bytes 946176
  846.2 360.3 %all-to-all-start.11 = ((bf16[32,10,3584]{2,1,0:T(8,128)(2,1)}), bf16[32,10,3584]{2,1,0:T(8,128)(2,1)}, u32[]{:S(2)}, u32[]{:S(2)}) async-start(bf16[32,10,3584]{2,1,0:T(8,128)(2,1)} %reshape.458), calls=%async_computation.11 | async-start | bytes 7340032 | tf_op jit(solution)/shard_map/all_to_all | solution.py:55
  852.6 276.9 %reduce-scatter.27.cloned.1.call-start = ((), (), s32[]{:S(2)}) async-start(), calls=%async_computation.22 | async-start | bytes 946176
  854.3 350.7 %reduce-scatter.29.cloned.1.call-start = ((), (), s32[]{:S(2)}) async-start(), calls=%async_computation.23 | async-start | bytes 946176
  856.0 355.1 %copy-start.24 = (bf16[32,3584]{1,0:T(8,128)(2,1)S(1)}, bf16[32,3584]{1,0:T(8,128)(2,1)}, u32[]{:S(2)}) copy-start(bf16[32,3584]{1,0:T(8,128)(2,1)} %copy-done.23) | copy-start | bytes 688132
  856.0 355.1 %copy-start.26 = (bf16[32,3584]{1,0:T(8,128)(2,1)S(1)}, bf16[32,3584]{1,0:T(8,128)(2,1)}, u32[]{:S(2)}) copy-start(bf16[32,3584]{1,0:T(8,128)(2,1)} %copy-done.25) | copy-start | bytes 688132
  856.0 355.1 %copy-start.28 = (bf16[32,3584]{1,0:T(8,128)(2,1)S(1)}, bf16[32,3584]{1,0:T(8,128)(2,1)}, u32[]{:S(2)}) copy-start(bf16[32,3584]{1,0:T(8,128)(2,1)} %copy-done.27) | copy-start | bytes 688132
  856.0 355.1 %copy-start.30 = (bf16[32,3584]{1,0:T(8,128)(2,1)S(1)}, bf16[32,3584]{1,0:T(8,128)(2,1)}, u32[]{:S(2)}) copy-start(bf16[32,3584]{1,0:T(8,128)(2,1)} %copy-done.29) | copy-start | bytes 688132
  (42 other events, 915.4 us)
Sparse Core Ops, SparseCore 0:
  684.3 101.5 reduce-scatter.18
  789.5 112.7 reduce-scatter.20
  905.9 72.5 reduce-scatter.22
  981.8 72.0 reduce-scatter.24
  1057.4 72.0 reduce-scatter.26
  1132.9 72.0 reduce-scatter.28
where the time goes:
time: 1230 us; the launch traced here: 1220 us
  waiting for transfers between devices  865 us (70%)
  starting transfers between devices  154 us (13%)
  matrix products  106 us (9%)
  local copies, waits for them, and re-layouts  69.4 us (6%)
  between operations  15.8 us (1%)
    unnamed x12, waiting for transfers between devices  345 us
    all_to_all x6, waiting for transfers between devices, run_layer(): lax.all_to_all(outgoing, 'expert', split_axis=0, concat_axis=0, tiled=True)  272 us
    all_to_all x6, waiting for transfers between devices, run_layer(): lax.all_to_all(finished.reshape(source_count, item_count, feature_count),...  227 us
    ppermute x10, starting transfers between devices, passed_along(): lax.ppermute(value, axis, [(source, source + steps) for source in range(f...  75.6 us
    dot_general x4, matrix products, expert_rows(): jnp.dot(hidden, down_mat, preferred_element_type=jnp.float32)  44.7 us
    all_to_all x6, starting transfers between devices, run_layer(): lax.all_to_all(finished.reshape(source_count, item_count, feature_count),...  39.7 us
    all_to_all x6, starting transfers between devices, run_layer(): lax.all_to_all(outgoing, 'expert', split_axis=0, concat_axis=0, tiled=True)  37.8 us
    dot_general x6, matrix products, run_layer(): combined = jnp.dot(weighted, flat_returned, precision=lax.Precision.HIGHEST)  27.6 us
  transfers between devices with their start and end apart: 28, of which 26 were waited for; matrix products, arithmetic and copies ran while one was open for 4% of the time, Pallas kernels for 0%

commit v1 on v0

--- a/solution.py
+++ b/solution.py
@@ -82,6 +82,15 @@
     return jnp.einsum("td,tr->dr", row_source, tangents, preferred_element_type=jnp.float32)
 
 
+def summed_grad(partial_grad, expert_count, own_rows):
+    rope_width = partial_grad.shape[1]
+    halves = partial_grad.reshape(expert_count, 2, own_rows // 2, rope_width)
+    paired = jnp.concatenate([halves[:, 0], halves[:, 1]], axis=-1).astype(jnp.bfloat16)
+    gathered = lax.all_to_all(paired, "expert", split_axis=0, concat_axis=0, tiled=True)
+    total = jnp.sum(gathered.astype(jnp.float32), axis=0)
+    return jnp.concatenate([total[:, :rope_width], total[:, rope_width:]], axis=0)
+
+
 def on_device(
     down_tokens,
     up_tokens,
@@ -100,7 +109,6 @@
     segment_pos = lax.axis_index("pipe")
     micro_count = down_tokens.shape[0]
     feature_count = down_tokens.shape[2]
-    rope_width = key_cotangent.shape[4]
     own_rows = feature_count // expert_count
     norm_scale = norm_gain[0]
     weights = (w_gate[0, 0], w_up[0, 0], w_down[0, 0])
@@ -109,7 +117,8 @@
     from_next = jnp.zeros_like(up_tokens[0])
     down_states = jnp.zeros_like(down_tokens)
     up_states = jnp.zeros_like(up_tokens)
-    key_grad_acc = jnp.zeros((own_rows, rope_width), jnp.float32)
+    normed_rows = []
+    tangent_rows = []
     micro_slots = jnp.arange(micro_count, dtype=jnp.int32)
     for step_index in range(total_steps):
         lag_down = step_index - segment_pos
@@ -133,15 +142,14 @@
         )
         tangent = jnp.where(down_on, key_cotangent[0, 0, down_mb], key_cotangent[0, 1, up_mb])
         tangent = tangent * active.astype(tangent.dtype)
-        key_grad_acc = key_grad_acc + lax.psum_scatter(
-            grad_term(normed, tangent).astype(jnp.bfloat16),
-            "expert",
-            scatter_dimension=0,
-            tiled=True,
-        ).astype(jnp.float32)
+        normed_rows.append(normed)
+        tangent_rows.append(tangent)
         if step_index + 1 < total_steps:
             from_prior, from_next = pass_on(output)
-    return (down_states[None], up_states[None], key_grad_acc[None])
+    key_grad = summed_grad(
+        grad_term(jnp.concatenate(normed_rows), jnp.concatenate(tangent_rows)), expert_count, own_rows
+    )
+    return (down_states[None], up_states[None], key_grad[None])
 
 
 def solution(mesh):

time: 1230 us -> 915 us (0.74)
  waiting for transfers between devices: 865 us -> 563 us
  between operations: 15.8 us -> 2.59 us
    unnamed x12 -> x0, waiting for transfers between devices: 345 us -> none
    all_to_all x6, waiting for transfers between devices: 227 us -> 273 us  [run_layer(): lax.all_to_all(finished.reshape(source_count, item_count, feature_count),...]
  transfers between devices with their start and end apart: 28 -> 23, of which waited for: 26 -> 22; matrix products, arithmetic and copies ran while one was open for 4% -> 4% of each run, Pallas kernels for 0% -> 0%
where the time goes in v1:
time: 915 us; the launch traced here: 906 us
  waiting for transfers between devices  563 us (62%)
  starting transfers between devices  160 us (17%)
  matrix products  104 us (11%)
  local copies, waits for them, and re-layouts  64 us (7%)
  other arithmetic  11.4 us (1%)
    all_to_all x6, waiting for transfers between devices, run_layer(): lax.all_to_all(finished.reshape(source_count, item_count, feature_count),...  273 us
    all_to_all x6, waiting for transfers between devices, run_layer(): lax.all_to_all(outgoing, 'expert', split_axis=0, concat_axis=0, tiled=True)  267 us
    ppermute x10, starting transfers between devices, passed_along(): lax.ppermute(value, axis, [(source, source + steps) for source in range(f...  75.6 us
    dot_general x4, matrix products, expert_rows(): jnp.dot(hidden, down_mat, preferred_element_type=jnp.float32)  44.6 us
    all_to_all x6, starting transfers between devices, run_layer(): lax.all_to_all(finished.reshape(source_count, item_count, feature_count),...  40.6 us
    all_to_all x6, starting transfers between devices, run_layer(): lax.all_to_all(outgoing, 'expert', split_axis=0, concat_axis=0, tiled=True)  38 us
    dot_general x6, matrix products, run_layer(): combined = jnp.dot(weighted, flat_returned, precision=lax.Precision.HIGHEST)  27.6 us
    dot_general x4, matrix products, expert_rows(): gate_act = jnp.dot(row_block, gate_mat, preferred_element_type=jnp.float32)  26.7 us
  transfers between devices with their start and end apart: 23, of which 22 were waited for; matrix products, arithmetic and copies ran while one was open for 4% of the time, Pallas kernels for 0%

profile of v1, /device:TPU:0, one launch (start us, length us, event | category | flops | bytes accessed | tf_op | source)
XLA Modules:
  0.0 905.5 jit_solution(5027023156629984440)
XLA Ops:
  8.8 7.5 all-to-all-start
  16.3 46.1 %all-to-all-done = bf16[32,10,3584]{2,1,0:T(8,128)(2,1)} async-done(((bf16[32,10,3584]{2,1,0:T(8,128)(2,1)}), bf16[32,10,3584]{2,1,0:T(8,128)(2,1)}, u32[]{:S(2)}, u32[]{:S(2)}) %all-to-all-start) | async-done | bytes 2293792 | tf_op jit(solution)/shard_map/all_to_all | solution.py:51
  62.5 22.4 %conditional.6 = (bf16[320,3584]{1,0:T(8,128)(2,1)S(1)}) conditional(s32[]{:T(128)} %convert_element_type.233, () %tuple.44, (bf16[32,10,3584]{2,1,0:T(8,128)(2,1)}, bf16[3584,1024]{1,0:T(8,128)(2,1)}, bf16[3584,1024]{1,0:T(8,128)(2,1)}, bf16[1024,3584]{1,0:T(8,128)(2,1)}) %tuple.124), branch_computations={%region_4.5_spmd, %region_5.6_spmd} | conditional | flops 7049543680 | bytes 45285412 | solution.py:54
  67.0 6.7 fusion.186
  73.7 11.2 %convolution_convert_fusion = bf16[320,3584]{1,0:T(8,128)(2,1)S(1)} fusion(bf16[1024,3584]{1,0:T(8,128)(2,1)} %get-tuple-element.75, bf16[320,3584]{1,0:T(8,128)(2,1)} %copy-done.2, bf16[3584,1024]{1,0:T(8,128)(2,1)} %get-tuple-element.74, f32[320,1024]{1,0:T(8,128)} %fusion.186), kind=kOutput, calls=%fused_computation | convolution fusion | flops 4700733440 | bytes 20578304 | tf_op jit(solution)/shard_map/cond/branch_1_fun/dot_general | solution.py:27
  87.4 6.6 all-to-all-start.1
  95.0 45.2 %all-to-all-done.1 = bf16[32,10,3584]{2,1,0:T(8,128)(2,1)} async-done(((bf16[32,10,3584]{2,1,0:T(8,128)(2,1)}), bf16[32,10,3584]{2,1,0:T(8,128)(2,1)}, u32[]{:S(2)}, u32[]{:S(2)}) %all-to-all-start.1) | async-done | bytes 2293792 | tf_op jit(solution)/shard_map/all_to_all | solution.py:55
  166.1 46.1 %all-to-all-done.2 = bf16[32,10,3584]{2,1,0:T(8,128)(2,1)} async-done(((bf16[32,10,3584]{2,1,0:T(8,128)(2,1)}), bf16[32,10,3584]{2,1,0:T(8,128)(2,1)}, u32[]{:S(2)}, u32[]{:S(2)}) %all-to-all-start.2) | async-done | bytes 2293792 | tf_op jit(solution)/shard_map/all_to_all | solution.py:51
  215.0 6.6 all-to-all-start.3
  221.9 45.8 %all-to-all-done.3 = bf16[32,10,3584]{2,1,0:T(8,128)(2,1)} async-done(((bf16[32,10,3584]{2,1,0:T(8,128)(2,1)}), bf16[32,10,3584]{2,1,0:T(8,128)(2,1)}, u32[]{:S(2)}, u32[]{:S(2)}) %all-to-all-start.3) | async-done | bytes 2293792 | tf_op jit(solution)/shard_map/all_to_all | solution.py:55
  273.7 27.2 %collective-permute-start.2 = (bf16[32,3584]{1,0:T(8,128)(2,1)S(1)}, bf16[32,3584]{1,0:T(8,128)(2,1)S(1)}, u32[]{:S(2)}, u32[]{:S(2)}) collective-permute-start(bf16[32,3584]{1,0:T(8,128)(2,1)S(1)} %fusion.22), channel_id=1, source_target_pairs={{0,32},{32,64},{64,96},{1,33},{33,65},{65,97},{2,34},{34,66},{66,9... | collective-permute-start | bytes 688136 | tf_op jit(solution)/shard_map/ppermute | solution.py:14
  316.6 46.1 %all-to-all-done.4 = bf16[32,10,3584]{2,1,0:T(8,128)(2,1)} async-done(((bf16[32,10,3584]{2,1,0:T(8,128)(2,1)}), bf16[32,10,3584]{2,1,0:T(8,128)(2,1)}, u32[]{:S(2)}, u32[]{:S(2)}) %all-to-all-start.4) | async-done | bytes 2293792 | tf_op jit(solution)/shard_map/all_to_all | solution.py:51
  362.7 22.4 %conditional.8 = (bf16[320,3584]{1,0:T(8,128)(2,1)S(1)}) conditional(s32[]{:T(128)} %convert_element_type.249, () %tuple.48, (bf16[32,10,3584]{2,1,0:T(8,128)(2,1)}, bf16[3584,1024]{1,0:T(8,128)(2,1)}, bf16[3584,1024]{1,0:T(8,128)(2,1)}, bf16[1024,3584]{1,0:T(8,128)(2,1)}) %tuple.126), branch_computations={%region_16.17_spmd, %region_17.18_spmd} | conditional | flops 7049543680 | bytes 45285412 | solution.py:54
  367.3 6.7 fusion.188
  373.9 11.2 %convolution_convert_fusion.2 = bf16[320,3584]{1,0:T(8,128)(2,1)S(1)} fusion(bf16[1024,3584]{1,0:T(8,128)(2,1)} %get-tuple-element.83, bf16[320,3584]{1,0:T(8,128)(2,1)} %copy-done.4, bf16[3584,1024]{1,0:T(8,128)(2,1)} %get-tuple-element.82, f32[320,1024]{1,0:T(8,128)} %fusion.188), kind=kOutput, calls=%fused_computation.8 | convolution fusion | flops 4700733440 | bytes 20578304 | tf_op jit(solution)/shard_map/cond/branch_1_fun/dot_general | solution.py:27
  387.7 6.8 all-to-all-start.5
  394.8 45.9 %all-to-all-done.5 = bf16[32,10,3584]{2,1,0:T(8,128)(2,1)} async-done(((bf16[32,10,3584]{2,1,0:T(8,128)(2,1)}), bf16[32,10,3584]{2,1,0:T(8,128)(2,1)}, u32[]{:S(2)}, u32[]{:S(2)}) %all-to-all-start.5) | async-done | bytes 2293792 | tf_op jit(solution)/shard_map/all_to_all | solution.py:55
  467.3 46.1 %all-to-all-done.6 = bf16[32,10,3584]{2,1,0:T(8,128)(2,1)} async-done(((bf16[32,10,3584]{2,1,0:T(8,128)(2,1)}), bf16[32,10,3584]{2,1,0:T(8,128)(2,1)}, u32[]{:S(2)}, u32[]{:S(2)}) %all-to-all-start.6) | async-done | bytes 2293792 | tf_op jit(solution)/shard_map/all_to_all | solution.py:51
  513.4 22.4 %conditional.9 = (bf16[320,3584]{1,0:T(8,128)(2,1)S(1)}) conditional(s32[]{:T(128)} %convert_element_type.257, () %tuple.50, (bf16[32,10,3584]{2,1,0:T(8,128)(2,1)}, bf16[3584,1024]{1,0:T(8,128)(2,1)}, bf16[3584,1024]{1,0:T(8,128)(2,1)}, bf16[1024,3584]{1,0:T(8,128)(2,1)}) %tuple.127), branch_computations={%region_22.23_spmd, %region_23.24_spmd} | conditional | flops 7049543680 | bytes 45285412 | solution.py:54
  518.0 6.7 fusion.189
  524.7 11.2 %convolution_convert_fusion.3 = bf16[320,3584]{1,0:T(8,128)(2,1)S(1)} fusion(bf16[1024,3584]{1,0:T(8,128)(2,1)} %get-tuple-element.87, bf16[320,3584]{1,0:T(8,128)(2,1)} %copy-done.5, bf16[3584,1024]{1,0:T(8,128)(2,1)} %get-tuple-element.86, f32[320,1024]{1,0:T(8,128)} %fusion.189), kind=kOutput, calls=%fused_computation.12 | convolution fusion | flops 4700733440 | bytes 20578304 | tf_op jit(solution)/shard_map/cond/branch_1_fun/dot_general | solution.py:27
  538.4 6.6 all-to-all-start.7
  545.4 45.8 %all-to-all-done.7 = bf16[32,10,3584]{2,1,0:T(8,128)(2,1)} async-done(((bf16[32,10,3584]{2,1,0:T(8,128)(2,1)}), bf16[32,10,3584]{2,1,0:T(8,128)(2,1)}, u32[]{:S(2)}, u32[]{:S(2)}) %all-to-all-start.7) | async-done | bytes 2293792 | tf_op jit(solution)/shard_map/all_to_all | solution.py:55
  619.2 44.9 %all-to-all-done.8 = bf16[32,10,3584]{2,1,0:T(8,128)(2,1)} async-done(((bf16[32,10,3584]{2,1,0:T(8,128)(2,1)}), bf16[32,10,3584]{2,1,0:T(8,128)(2,1)}, u32[]{:S(2)}, u32[]{:S(2)}) %all-to-all-start.8) | async-done | bytes 2293792 | tf_op jit(solution)/shard_map/all_to_all | solution.py:51
  674.0 45.5 %all-to-all-done.9 = bf16[32,10,3584]{2,1,0:T(8,128)(2,1)} async-done(((bf16[32,10,3584]{2,1,0:T(8,128)(2,1)}), bf16[32,10,3584]{2,1,0:T(8,128)(2,1)}, u32[]{:S(2)}, u32[]{:S(2)}) %all-to-all-start.9) | async-done | bytes 2293792 | tf_op jit(solution)/shard_map/all_to_all | solution.py:55
  725.4 27.2 %collective-permute-start.8 = (bf16[32,3584]{1,0:T(8,128)(2,1)S(1)}, bf16[32,3584]{1,0:T(8,128)(2,1)S(1)}, u32[]{:S(2)}, u32[]{:S(2)}) collective-permute-start(bf16[32,3584]{1,0:T(8,128)(2,1)S(1)} %fusion.19), channel_id=1, source_target_pairs={{0,32},{32,64},{64,96},{1,33},{33,65},{65,97},{2,34},{34,66},{66,9... | collective-permute-start | bytes 688136 | tf_op jit(solution)/shard_map/ppermute | solution.py:14
  776.0 38.0 %all-to-all-done.10 = bf16[32,10,3584]{2,1,0:T(8,128)(2,1)} async-done(((bf16[32,10,3584]{2,1,0:T(8,128)(2,1)}), bf16[32,10,3584]{2,1,0:T(8,128)(2,1)}, u32[]{:S(2)}, u32[]{:S(2)}) %all-to-all-start.10) | async-done | bytes 2293792 | tf_op jit(solution)/shard_map/all_to_all | solution.py:51
  820.2 22.6 %conditional.11 = (bf16[320,3584]{1,0:T(8,128)(2,1)S(1)}) conditional(s32[]{:T(128)} %convert_element_type.273, () %tuple.54, (bf16[32,10,3584]{2,1,0:T(8,128)(2,1)}, bf16[3584,1024]{1,0:T(8,128)(2,1)}, bf16[3584,1024]{1,0:T(8,128)(2,1)}, bf16[1024,3584]{1,0:T(8,128)(2,1)}) %tuple.129), branch_computations={%region_34.35_spmd, %region_35.36_spmd} | conditional | flops 7049543680 | bytes 45285412 | solution.py:54
  825.0 6.7 fusion.191
  831.7 11.2 %convolution_convert_fusion.5 = bf16[320,3584]{1,0:T(8,128)(2,1)S(1)} fusion(bf16[1024,3584]{1,0:T(8,128)(2,1)} %get-tuple-element.95, bf16[320,3584]{1,0:T(8,128)(2,1)} %copy-done.7, bf16[3584,1024]{1,0:T(8,128)(2,1)} %get-tuple-element.94, f32[320,1024]{1,0:T(8,128)} %fusion.191), kind=kOutput, calls=%fused_computation.20 | convolution fusion | flops 4700733440 | bytes 20578304 | tf_op jit(solution)/shard_map/cond/branch_1_fun/dot_general | solution.py:27
  845.5 7.5 all-to-all-start.11
  854.2 44.9 %all-to-all-done.11 = bf16[32,10,3584]{2,1,0:T(8,128)(2,1)} async-done(((bf16[32,10,3584]{2,1,0:T(8,128)(2,1)}), bf16[32,10,3584]{2,1,0:T(8,128)(2,1)}, u32[]{:S(2)}, u32[]{:S(2)}) %all-to-all-start.11) | async-done | bytes 2293792 | tf_op jit(solution)/shard_map/all_to_all | solution.py:55
  (238 shorter events, 194.9 us)
Async XLA Ops:
  8.8 53.7 %all-to-all-start = ((bf16[32,10,3584]{2,1,0:T(8,128)(2,1)}), bf16[32,10,3584]{2,1,0:T(8,128)(2,1)}, u32[]{:S(2)}, u32[]{:S(2)}) async-start(bf16[32,10,3584]{2,1,0:T(8,128)(2,1)} %copy.139), calls=%async_computation | async-start | bytes 7340032 | tf_op jit(solution)/shard_map/all_to_all | solution.py:51
  87.4 52.8 %all-to-all-start.1 = ((bf16[32,10,3584]{2,1,0:T(8,128)(2,1)}), bf16[32,10,3584]{2,1,0:T(8,128)(2,1)}, u32[]{:S(2)}, u32[]{:S(2)}) async-start(bf16[32,10,3584]{2,1,0:T(8,128)(2,1)} %reshape.445), calls=%async_computation.1 | async-start | bytes 7340032 | tf_op jit(solution)/shard_map/all_to_all | solution.py:55
  94.1 61.0 %copy-start = (bf16[2,32,3584]{2,1,0:T(8,128)(2,1)S(1)}, bf16[2,32,3584]{2,1,0:T(8,128)(2,1)}, u32[]{:S(2)}) copy-start(bf16[2,32,3584]{2,1,0:T(8,128)(2,1)} %param.24) | copy-start | bytes 1376260
  94.1 61.0 %copy-start.1 = (bf16[2,32,3584]{2,1,0:T(8,128)(2,1)S(1)}, bf16[2,32,3584]{2,1,0:T(8,128)(2,1)}, u32[]{:S(2)}) copy-start(bf16[2,32,3584]{2,1,0:T(8,128)(2,1)} %param.23) | copy-start | bytes 1376260
  144.8 9.1 %collective-permute-start.1 = (bf16[32,3584]{1,0:T(8,128)(2,1)S(1)}, bf16[32,3584]{1,0:T(8,128)(2,1)S(1)}, u32[]{:S(2)}, u32[]{:S(2)}) collective-permute-start(bf16[32,3584]{1,0:T(8,128)(2,1)S(1)} %fusion.23), channel_id=1, source_target_pairs={{32,0},{64,32},{96,64},{33,1},{65,33},{97,65},{34,2},{66,34},{98,6... | collective-permute-start | bytes 688136 | tf_op jit(solution)/shard_map/ppermute | solution.py:14
  146.1 9.0 collective-permute-start
  160.0 52.2 %all-to-all-start.2 = ((bf16[32,10,3584]{2,1,0:T(8,128)(2,1)}), bf16[32,10,3584]{2,1,0:T(8,128)(2,1)}, u32[]{:S(2)}, u32[]{:S(2)}) async-start(bf16[32,10,3584]{2,1,0:T(8,128)(2,1)} %copy.144), calls=%async_computation.2 | async-start | bytes 7340032 | tf_op jit(solution)/shard_map/all_to_all | solution.py:51
  215.0 52.8 %copy-start.9 = (bf16[32,3584]{1,0:T(8,128)(2,1)S(1)}, bf16[32,3584]{1,0:T(8,128)(2,1)}, u32[]{:S(2)}) copy-start(bf16[32,3584]{1,0:T(8,128)(2,1)} %copy-done.8) | copy-start | bytes 688132
  215.0 52.8 %all-to-all-start.3 = ((bf16[32,10,3584]{2,1,0:T(8,128)(2,1)}), bf16[32,10,3584]{2,1,0:T(8,128)(2,1)}, u32[]{:S(2)}, u32[]{:S(2)}) async-start(bf16[32,10,3584]{2,1,0:T(8,128)(2,1)} %reshape.446), calls=%async_computation.3 | async-start | bytes 7340032 | tf_op jit(solution)/shard_map/all_to_all | solution.py:55
  272.4 32.1 %collective-permute-start.3 = (bf16[32,3584]{1,0:T(8,128)(2,1)S(1)}, bf16[32,3584]{1,0:T(8,128)(2,1)S(1)}, u32[]{:S(2)}, u32[]{:S(2)}) collective-permute-start(bf16[32,3584]{1,0:T(8,128)(2,1)S(1)} %fusion.22), channel_id=1, source_target_pairs={{32,0},{64,32},{96,64},{33,1},{65,33},{97,65},{34,2},{66,34},{98,6... | collective-permute-start | bytes 688136 | tf_op jit(solution)/shard_map/ppermute | solution.py:14
  273.7 31.9 %collective-permute-start.2 = (bf16[32,3584]{1,0:T(8,128)(2,1)S(1)}, bf16[32,3584]{1,0:T(8,128)(2,1)S(1)}, u32[]{:S(2)}, u32[]{:S(2)}) collective-permute-start(bf16[32,3584]{1,0:T(8,128)(2,1)S(1)} %fusion.22), channel_id=1, source_target_pairs={{0,32},{32,64},{64,96},{1,33},{33,65},{65,97},{2,34},{34,66},{66,9... | collective-permute-start | bytes 688136 | tf_op jit(solution)/shard_map/ppermute | solution.py:14
  310.5 52.2 %all-to-all-start.4 = ((bf16[32,10,3584]{2,1,0:T(8,128)(2,1)}), bf16[32,10,3584]{2,1,0:T(8,128)(2,1)}, u32[]{:S(2)}, u32[]{:S(2)}) async-start(bf16[32,10,3584]{2,1,0:T(8,128)(2,1)} %copy.149), calls=%async_computation.4 | async-start | bytes 7340032 | tf_op jit(solution)/shard_map/all_to_all | solution.py:51
  387.7 53.0 %copy-start.12 = (bf16[32,3584]{1,0:T(8,128)(2,1)S(1)}, bf16[32,3584]{1,0:T(8,128)(2,1)}, u32[]{:S(2)}) copy-start(bf16[32,3584]{1,0:T(8,128)(2,1)} %copy-done.11) | copy-start | bytes 688132
  387.7 53.0 %all-to-all-start.5 = ((bf16[32,10,3584]{2,1,0:T(8,128)(2,1)}), bf16[32,10,3584]{2,1,0:T(8,128)(2,1)}, u32[]{:S(2)}, u32[]{:S(2)}) async-start(bf16[32,10,3584]{2,1,0:T(8,128)(2,1)} %reshape.447), calls=%async_computation.5 | async-start | bytes 7340032 | tf_op jit(solution)/shard_map/all_to_all | solution.py:55
  445.3 9.8 %collective-permute-start.5 = (bf16[32,3584]{1,0:T(8,128)(2,1)S(1)}, bf16[32,3584]{1,0:T(8,128)(2,1)S(1)}, u32[]{:S(2)}, u32[]{:S(2)}) collective-permute-start(bf16[32,3584]{1,0:T(8,128)(2,1)S(1)} %fusion.21), channel_id=1, source_target_pairs={{32,0},{64,32},{96,64},{33,1},{65,33},{97,65},{34,2},{66,34},{98,6... | collective-permute-start | bytes 688136 | tf_op jit(solution)/shard_map/ppermute | solution.py:14
  446.6 9.7 %collective-permute-start.4 = (bf16[32,3584]{1,0:T(8,128)(2,1)S(1)}, bf16[32,3584]{1,0:T(8,128)(2,1)S(1)}, u32[]{:S(2)}, u32[]{:S(2)}) collective-permute-start(bf16[32,3584]{1,0:T(8,128)(2,1)S(1)} %fusion.21), channel_id=1, source_target_pairs={{0,32},{32,64},{64,96},{1,33},{33,65},{65,97},{2,34},{34,66},{66,9... | collective-permute-start | bytes 688136 | tf_op jit(solution)/shard_map/ppermute | solution.py:14
  461.2 52.2 %all-to-all-start.6 = ((bf16[32,10,3584]{2,1,0:T(8,128)(2,1)}), bf16[32,10,3584]{2,1,0:T(8,128)(2,1)}, u32[]{:S(2)}, u32[]{:S(2)}) async-start(bf16[32,10,3584]{2,1,0:T(8,128)(2,1)} %copy.154), calls=%async_computation.6 | async-start | bytes 7340032 | tf_op jit(solution)/shard_map/all_to_all | solution.py:51
  538.4 52.8 %copy-start.15 = (bf16[32,3584]{1,0:T(8,128)(2,1)S(1)}, bf16[32,3584]{1,0:T(8,128)(2,1)}, u32[]{:S(2)}) copy-start(bf16[32,3584]{1,0:T(8,128)(2,1)} %copy-done.14) | copy-start | bytes 688132
  538.4 52.8 %all-to-all-start.7 = ((bf16[32,10,3584]{2,1,0:T(8,128)(2,1)}), bf16[32,10,3584]{2,1,0:T(8,128)(2,1)}, u32[]{:S(2)}, u32[]{:S(2)}) async-start(bf16[32,10,3584]{2,1,0:T(8,128)(2,1)} %reshape.448), calls=%async_computation.7 | async-start | bytes 7340032 | tf_op jit(solution)/shard_map/all_to_all | solution.py:55
  595.8 9.8 %collective-permute-start.7 = (bf16[32,3584]{1,0:T(8,128)(2,1)S(1)}, bf16[32,3584]{1,0:T(8,128)(2,1)S(1)}, u32[]{:S(2)}, u32[]{:S(2)}) collective-permute-start(bf16[32,3584]{1,0:T(8,128)(2,1)S(1)} %fusion.20), channel_id=1, source_target_pairs={{32,0},{64,32},{96,64},{33,1},{65,33},{97,65},{34,2},{66,34},{98,6... | collective-permute-start | bytes 688136 | tf_op jit(solution)/shard_map/ppermute | solution.py:14
  597.1 9.7 %collective-permute-start.6 = (bf16[32,3584]{1,0:T(8,128)(2,1)S(1)}, bf16[32,3584]{1,0:T(8,128)(2,1)S(1)}, u32[]{:S(2)}, u32[]{:S(2)}) collective-permute-start(bf16[32,3584]{1,0:T(8,128)(2,1)S(1)} %fusion.20), channel_id=1, source_target_pairs={{0,32},{32,64},{64,96},{1,33},{33,65},{65,97},{2,34},{34,66},{66,9... | collective-permute-start | bytes 688136 | tf_op jit(solution)/shard_map/ppermute | solution.py:14
  611.8 52.3 %all-to-all-start.8 = ((bf16[32,10,3584]{2,1,0:T(8,128)(2,1)}), bf16[32,10,3584]{2,1,0:T(8,128)(2,1)}, u32[]{:S(2)}, u32[]{:S(2)}) async-start(bf16[32,10,3584]{2,1,0:T(8,128)(2,1)} %copy.159), calls=%async_computation.8 | async-start | bytes 7340032 | tf_op jit(solution)/shard_map/all_to_all | solution.py:51
  666.9 52.6 %copy-start.18 = (bf16[32,3584]{1,0:T(8,128)(2,1)S(1)}, bf16[32,3584]{1,0:T(8,128)(2,1)}, u32[]{:S(2)}) copy-start(bf16[32,3584]{1,0:T(8,128)(2,1)} %copy-done.17) | copy-start | bytes 688132
  666.9 52.6 %all-to-all-start.9 = ((bf16[32,10,3584]{2,1,0:T(8,128)(2,1)}), bf16[32,10,3584]{2,1,0:T(8,128)(2,1)}, u32[]{:S(2)}, u32[]{:S(2)}) async-start(bf16[32,10,3584]{2,1,0:T(8,128)(2,1)} %reshape.449), calls=%async_computation.9 | async-start | bytes 7340032 | tf_op jit(solution)/shard_map/all_to_all | solution.py:55
  673.5 79.2 %copy-start.16 = (bf16[32,3584]{1,0:T(8,128)(2,1)S(1)}, bf16[32,3584]{1,0:T(8,128)(2,1)}, u32[]{:S(2)}) copy-start(bf16[32,3584]{1,0:T(8,128)(2,1)} %copy-done.14) | copy-start | bytes 688132
  673.5 79.2 %copy-start.48 = (f32[32]{0:T(128)S(1)}, f32[32]{0:T(128)}, u32[]{:S(2)}) copy-start(f32[32]{0:T(128)} %copy-done.47) | copy-start | bytes 388
  724.1 32.1 %collective-permute-start.9 = (bf16[32,3584]{1,0:T(8,128)(2,1)S(1)}, bf16[32,3584]{1,0:T(8,128)(2,1)S(1)}, u32[]{:S(2)}, u32[]{:S(2)}) collective-permute-start(bf16[32,3584]{1,0:T(8,128)(2,1)S(1)} %fusion.19), channel_id=1, source_target_pairs={{32,0},{64,32},{96,64},{33,1},{65,33},{97,65},{34,2},{66,34},{98,6... | collective-permute-start | bytes 688136 | tf_op jit(solution)/shard_map/ppermute | solution.py:14
  725.4 32.0 %collective-permute-start.8 = (bf16[32,3584]{1,0:T(8,128)(2,1)S(1)}, bf16[32,3584]{1,0:T(8,128)(2,1)S(1)}, u32[]{:S(2)}, u32[]{:S(2)}) collective-permute-start(bf16[32,3584]{1,0:T(8,128)(2,1)S(1)} %fusion.19), channel_id=1, source_target_pairs={{0,32},{32,64},{64,96},{1,33},{33,65},{65,97},{2,34},{34,66},{66,9... | collective-permute-start | bytes 688136 | tf_op jit(solution)/shard_map/ppermute | solution.py:14
  761.7 52.4 %all-to-all-start.10 = ((bf16[32,10,3584]{2,1,0:T(8,128)(2,1)}), bf16[32,10,3584]{2,1,0:T(8,128)(2,1)}, u32[]{:S(2)}, u32[]{:S(2)}) async-start(bf16[32,10,3584]{2,1,0:T(8,128)(2,1)} %copy.164), calls=%async_computation.10 | async-start | bytes 7340032 | tf_op jit(solution)/shard_map/all_to_all | solution.py:51
  814.0 31.4 %all-to-all-start.12 = ((bf16[32,56,128]{2,1,0:T(8,128)(2,1)}), bf16[32,56,128]{2,1,0:T(8,128)(2,1)S(1)}, u32[]{:S(2)}, u32[]{:S(2)}) async-start(bf16[32,56,128]{2,1,0:T(8,128)(2,1)} %pad_maximum_fusion), calls=%async_computation.12 | async-start | bytes 917504 | tf_op jit(solution)/shard_map/all_to_all | solution.py:89
  845.5 53.7 %all-to-all-start.11 = ((bf16[32,10,3584]{2,1,0:T(8,128)(2,1)}), bf16[32,10,3584]{2,1,0:T(8,128)(2,1)}, u32[]{:S(2)}, u32[]{:S(2)}) async-start(bf16[32,10,3584]{2,1,0:T(8,128)(2,1)} %reshape.450), calls=%async_computation.11 | async-start | bytes 7340032 | tf_op jit(solution)/shard_map/all_to_all | solution.py:55
  853.0 50.8 %copy-start.22 = (bf16[32,3584]{1,0:T(8,128)(2,1)S(1)}, bf16[32,3584]{1,0:T(8,128)(2,1)}, u32[]{:S(2)}) copy-start(bf16[32,3584]{1,0:T(8,128)(2,1)} %copy-done.21) | copy-start | bytes 688132
  (40 other events, 510.9 us)
